TPU v7x, 32 devices: a whole 2x2x4 slice. The times are simulated.
32 devices in a mesh: leaf: 8 (over y, x, core), row: 4 (over z).
Axes of the slice: x: 2, y: 2, z: 4, core: 2. Of those that a mesh axis runs over, the one named last changes fastest.
Arguments:
- sources_root: float32 [64, 32, 128], P('leaf'), may hold values from -6 to 6
- sources_upper: float32 [64, 32, 128], P('leaf'), may hold values from -6 to 6
- sources_middle: float32 [64, 32, 128], P('leaf'), may hold values from -6 to 6
- sources_lower: float32 [64, 32, 128], P('leaf'), may hold values from -6 to 6
- inverse_root: float32 [64, 128, 8192], P('leaf', None, 'row'), may hold values from -4 to 4, as said below
- inverse_upper: float32 [64, 128, 4096], P('leaf', None, 'row'), may hold values from -4 to 4, as said below
- inverse_middle: float32 [64, 128, 2048], P('leaf', None, 'row'), may hold values from -4 to 4, as said below
- inverse_lower: float32 [64, 128, 1024], P('leaf', None, 'row'), may hold values from -4 to 4, as said below
- update_upper: float32 [128, 128, 4096], P('leaf', None, 'row'), may hold values from -0.046875 to 0.046875
- update_middle: float32 [256, 128, 2048], P('leaf', None, 'row'), may hold values from -0.0625 to 0.0625
- update_lower: float32 [256, 128, 1024], P('leaf', None, 'row'), may hold values from -0.09375 to 0.09375
- links_upper: int32 [128], P('leaf'), may hold values from 0 to 63, as said below
- links_middle: int32 [256], P('leaf'), may hold values from 0 to 127, as said below
- links_lower: int32 [256], P('leaf'), may hold values from 0 to 191, as said below
Outputs:
- adjoint_root: float32 [64, 32, 128], P('leaf')
- adjoint_upper: float32 [64, 32, 128], P('leaf')
- adjoint_middle: float32 [64, 32, 128], P('leaf')
- adjoint_lower: float32 [64, 32, 128], P('leaf')
Inputs may be any that keep to these rules, and one draw needn't show every extreme that they name: `inverse_root`: lower triangular: stored entry [g, t, p] is zero where g * 128 + t > p. `inverse_upper`: lower triangular: stored entry [g, t, p] is zero where (g % 32) * 128 + t > p. `inverse_middle`: lower triangular: stored entry [g, t, p] is zero where (g % 16) * 128 + t > p. `inverse_lower`: lower triangular: stored entry [g, t, p] is zero where (g % 8) * 128 + t > p. `links_upper`: the entries of one front are distinct and all belong to the root front. `links_middle`: the entries of one front are distinct and belong to the front's own ancestors (the root and its parent of level 1). `links_lower`: the entries of one front are distinct and belong to the front's own ancestors on levels 0 to 2.
All inputs are finite; a program needn't handle non-finite values.
Results may differ from a plain program's by a relative error of at most 0.00014.
Values sent between devices are 32-bit elements; how exact they have to be, the bound alone decides.
A program may use at most 128 MiB of HBM per device.

v0:
```python
import jax
import jax.numpy as jnp
from jax import lax
from jax.sharding import PartitionSpec as P

PIV_ROOT = 8192
BLOCK_ROWS = 128


TOP_PRECISION = lax.Precision.HIGHEST


def swapped(x, axis, stride):
    return lax.ppermute(x, axis, [(i, i ^ 1 << stride) for i in range(lax.axis_size(axis))])


def group_total(value_partial_sum, level_bits):
    for bit_index in range(level_bits):
        value_partial_sum = value_partial_sum + swapped(value_partial_sum, "leaf", bit_index)
    return value_partial_sum


def pending_share(stacked, level_bits, position):
    for bit_index in reversed(range(level_bits)):
        halfway = stacked.shape[0] // 2
        parity = jnp.right_shift(position, bit_index) % 2
        retained = jnp.where(parity == 1, stacked[halfway:], stacked[:halfway])
        handed = jnp.where(parity == 1, stacked[:halfway], stacked[halfway:])
        stacked = retained + swapped(handed, "leaf", bit_index)
    return stacked


def whole_front(stacked, level_bits, position):
    for bit_index in range(level_bits):
        partner = swapped(stacked, "leaf", bit_index)
        parity = jnp.right_shift(position, bit_index) % 2
        stacked = jnp.where(
            parity == 1,
            jnp.concatenate([partner, stacked], axis=0),
            jnp.concatenate([stacked, partner], axis=0),
        )
    return stacked


def choose_blocks(targets, upper_level, count):
    level_of = targets // (PIV_ROOT // BLOCK_ROWS)
    within = targets % count
    hits = (level_of == upper_level)[:, None] & (
        within[:, None] == jnp.arange(count, dtype=jnp.int32)[None, :]
    )
    return hits.astype(jnp.float32)


def body(
    sources_root,
    sources_upper,
    sources_middle,
    sources_lower,
    inverse_root,
    inverse_upper,
    inverse_middle,
    inverse_lower,
    update_upper,
    update_middle,
    update_lower,
    links_upper,
    links_middle,
    links_lower,
):
    sources = [sources_root, sources_upper, sources_middle, sources_lower]
    inverse_factor = [inverse_root, inverse_upper, inverse_middle, inverse_lower]
    update = [None, update_upper, update_middle, update_lower]
    links = [None, links_upper, links_middle, links_lower]
    leaf_bits = lax.axis_size("leaf").bit_length() - 1
    position = lax.axis_index("leaf")
    columns = sources_root.shape[1]
    counts = [(PIV_ROOT >> upper_level) // BLOCK_ROWS for upper_level in range(4)]
    pending = [
        jnp.zeros((counts[upper_level], columns, BLOCK_ROWS), jnp.float32)
        for upper_level in range(3)
    ]
    column_selectors = [None, None, None, None]
    forward = [None, None, None, None]
    for level_in_tree in (3, 2, 1, 0):
        level_bits = leaf_bits - level_in_tree
        source_vector = sources[level_in_tree]
        if level_in_tree < 3:
            arriving = pending_share(pending[level_in_tree], level_bits, position)
            arriving = lax.psum(arriving, "row")
            source_vector = source_vector - arriving
        value_partial_sum = jnp.einsum(
            "dkx,dek->ex", inverse_factor[level_in_tree], source_vector, precision=TOP_PRECISION
        )
        solved = group_total(value_partial_sum, level_bits)
        forward[level_in_tree] = solved
        if level_in_tree > 0:
            matrix_product = jnp.einsum(
                "ktp,rp->krt", update[level_in_tree], solved, precision=TOP_PRECISION
            )
            column_selectors[level_in_tree] = [
                choose_blocks(links[level_in_tree], upper_level, counts[upper_level])
                for upper_level in range(level_in_tree)
            ]
            for upper_level in range(level_in_tree):
                pending[upper_level] = pending[upper_level] + jnp.einsum(
                    "xs,xon->son",
                    column_selectors[level_in_tree][upper_level],
                    matrix_product,
                    precision=TOP_PRECISION,
                )
    solutions = [None, None, None, None]
    whole_fronts = [None, None, None]
    for level_in_tree in range(4):
        level_bits = leaf_bits - level_in_tree
        fixed_update = forward[level_in_tree]
        if level_in_tree > 0:
            gathered = jnp.einsum(
                "wq,qfx->wfx",
                column_selectors[level_in_tree][0],
                whole_fronts[0],
                precision=TOP_PRECISION,
            )
            for upper_level in range(1, level_in_tree):
                gathered = gathered + jnp.einsum(
                    "wq,qfx->wfx",
                    column_selectors[level_in_tree][upper_level],
                    whole_fronts[upper_level],
                    precision=TOP_PRECISION,
                )
            value_partial_sum = jnp.einsum(
                "ktp,krt->rp", update[level_in_tree], gathered, precision=TOP_PRECISION
            )
            fixed_update = fixed_update - group_total(value_partial_sum, level_bits)
        value_partial_sum = jnp.einsum(
            "hay,zy->hza", inverse_factor[level_in_tree], fixed_update, precision=TOP_PRECISION
        )
        solutions[level_in_tree] = lax.psum(value_partial_sum, "row")
        if level_in_tree < 3:
            whole_fronts[level_in_tree] = whole_front(
                solutions[level_in_tree], level_bits, position
            )
    return (solutions[0], solutions[1], solutions[2], solutions[3])


def solution(mesh):
    placed = (
        P("leaf", None, None),
        P("leaf", None, None),
        P("leaf", None, None),
        P("leaf", None, None),
        P("leaf", None, "row"),
        P("leaf", None, "row"),
        P("leaf", None, "row"),
        P("leaf", None, "row"),
        P("leaf", None, "row"),
        P("leaf", None, "row"),
        P("leaf", None, "row"),
        P("leaf"),
        P("leaf"),
        P("leaf"),
    )
    return jax.shard_map(
        body,
        mesh=mesh,
        in_specs=placed,
        out_specs=(
            P("leaf", None, None),
            P("leaf", None, None),
            P("leaf", None, None),
            P("leaf", None, None),
        ),
        check_vma=False,
    )
```

profile of v0, /device:TPU:0, one launch (start us, length us, event | category | flops | bytes accessed | tf_op | source)
XLA Modules:
  0.0 461.7 jit_solution(5404235102363132959)
XLA Ops:
  10.6 5.6 %convolution_bitcast_fusion.1 = f32[32,32,128]{2,1,0:T(8,128)S(1)} fusion(f32[32,256,1]{1,0,2:T(8,128)S(1)} %fusion.90, f32[32,128,256]{2,1,0:T(8,128)} %param.24), kind=kOutput, calls=%fused_computation.3 | convolution fusion | flops 402653184 | bytes 4751360 | tf_op jit(solution)/shard_map/ktp,rp->krt/dot_general | solution.py:97
  19.8 37.1 %all-reduce.8.cloned.1.call-done = f32[8,32,128]{2,0,1:T(8,128)} async-done(((f32[8,32,128]{2,0,1:T(8,128)}), f32[8,32,128]{2,0,1:T(8,128)}) %all-reduce.8.cloned.1.call-update) | async-done | bytes 131088 | tf_op jit(solution)/shard_map/psum | solution.py:89
  60.5 9.9 %convolution_bitcast_fusion.2 = f32[32,32,128]{2,1,0:T(8,128)S(1)} fusion(f32[32,128,512]{2,1,0:T(8,128)} %param.23, f32[32,512]{1,0:T(8,128)S(1)} %add.134), kind=kOutput, calls=%fused_computation.4 | convolution fusion | flops 805306368 | bytes 8978432 | tf_op jit(solution)/shard_map/ktp,rp->krt/dot_general | solution.py:97
  74.6 5.0 %collective-permute-done.2 = f32[16,32,128]{2,0,1:T(8,128)S(1)} collective-permute-done((f32[16,32,128]{2,0,1:T(8,128)S(1)}, f32[16,32,128]{2,0,1:T(8,128)S(1)}, u32[]{:S(2)}, u32[]{:S(2)}) %collective-permute-start.2) | collective-permute-done | bytes 262176 | tf_op jit(solution)/shard_map/ppermute | solution.py:14
  82.0 34.2 %all-reduce.10.cloned.1.call-done = f32[8,32,128]{2,0,1:T(8,128)} async-done(((f32[8,32,128]{2,0,1:T(8,128)}), f32[8,32,128]{2,0,1:T(8,128)}) %all-reduce.10.cloned.1.call-update) | async-done | bytes 131088 | tf_op jit(solution)/shard_map/psum | solution.py:89
  128.6 10.0 %fusion.30 = f32[32,16,128]{2,0,1:T(8,128)S(1)} fusion(f32[16,128,1024]{2,1,0:T(8,128)} %param.22, f32[32,1024]{1,0:T(8,128)S(1)} %add.143), kind=kOutput, calls=%fused_computation.60 | convolution fusion | flops 805306368 | bytes 8781824 | tf_op jit(solution)/shard_map/ktp,rp->krt/dot_general | solution.py:97
  140.9 11.7 %collective-permute-done.6 = f32[32,32,128]{2,0,1:T(8,128)S(1)} collective-permute-done((f32[32,32,128]{2,0,1:T(8,128)S(1)}, f32[32,32,128]{2,0,1:T(8,128)S(1)}, u32[]{:S(2)}, u32[]{:S(2)}) %collective-permute-start.6) | collective-permute-done | bytes 524320 | tf_op jit(solution)/shard_map/ppermute | solution.py:14
  154.3 5.2 %collective-permute-done.7 = f32[16,32,128]{2,0,1:T(8,128)S(1)} collective-permute-done((f32[16,32,128]{2,0,1:T(8,128)S(1)}, f32[16,32,128]{2,0,1:T(8,128)S(1)}, u32[]{:S(2)}, u32[]{:S(2)}) %collective-permute-start.7) | collective-permute-done | bytes 262176 | tf_op jit(solution)/shard_map/ppermute | solution.py:14
  161.7 34.4 %all-reduce.12.cloned.1.call-done = f32[8,32,128]{2,0,1:T(8,128)} async-done(((f32[8,32,128]{2,0,1:T(8,128)}), f32[8,32,128]{2,0,1:T(8,128)}) %all-reduce.12.cloned.1.call-update) | async-done | bytes 131088 | tf_op jit(solution)/shard_map/psum | solution.py:89
  197.1 7.2 %convolution_bitcast_fusion = f32[32,2048]{1,0:T(8,128)S(1)} fusion(f32[8,128,2048]{2,1,0:T(8,128)} %param.18, f32[8,32,128]{2,0,1:T(8,128)S(1)} %copy_subtract_fusion), kind=kOutput, calls=%fused_computation | convolution fusion | flops 805306368 | bytes 8781824 | tf_op jit(solution)/shard_map/dkx,dek->ex/dot_general | solution.py:91
  207.5 6.9 %collective-permute-done.10 = f32[32,2048]{1,0:T(8,128)S(1)} collective-permute-done((f32[32,2048]{1,0:T(8,128)S(1)}, f32[32,2048]{1,0:T(8,128)S(1)}, u32[]{:S(2)}, u32[]{:S(2)}) %collective-permute-start.10) | collective-permute-done | bytes 262176 | tf_op jit(solution)/shard_map/ppermute | solution.py:14
  215.9 6.0 %collective-permute-done.11 = f32[32,2048]{1,0:T(8,128)S(1)} collective-permute-done((f32[32,2048]{1,0:T(8,128)S(1)}, f32[32,2048]{1,0:T(8,128)S(1)}, u32[]{:S(2)}, u32[]{:S(2)}) %collective-permute-start.11) | collective-permute-done | bytes 262176 | tf_op jit(solution)/shard_map/ppermute | solution.py:14
  221.9 10.6 %convolution_bitcast_fusion.6 = f32[8,32,128]{2,1,0:T(8,128)} fusion(f32[8,128,2048]{2,1,0:T(8,128)} %param.18, f32[32,2048]{1,0:T(8,128)S(1)} %add.149, f32[32,2048]{1,0:T(8,128)S(1)} %collective-permute-done.11), kind=kOutput, calls=%fused_computation.9 | convolution fusion | flops 805371904 | bytes 9043968 | tf_op jit(solution)/shard_map/hay,zy->hza/dot_general | solution.py:134
  232.8 34.2 %all-reduce.14.cloned.1.call-done = f32[8,32,128]{2,1,0:T(8,128)} async-done(((f32[8,32,128]{2,1,0:T(8,128)}), f32[8,32,128]{2,1,0:T(8,128)}) %all-reduce.14.cloned.1.call-update) | async-done | bytes 131088 | tf_op jit(solution)/shard_map/psum | solution.py:137
  271.1 6.9 %collective-permute-done.13 = f32[16,32,128]{2,1,0:T(8,128)S(1)} collective-permute-done((f32[16,32,128]{2,1,0:T(8,128)S(1)}, f32[16,32,128]{2,1,0:T(8,128)S(1)}, u32[]{:S(2)}, u32[]{:S(2)}) %collective-permute-start.13) | collective-permute-done | bytes 262176 | tf_op jit(solution)/shard_map/ppermute | solution.py:14
  279.6 11.7 %collective-permute-done.14 = f32[32,32,128]{2,1,0:T(8,128)S(1)} collective-permute-done((f32[32,32,128]{2,1,0:T(8,128)S(1)}, f32[32,32,128]{2,1,0:T(8,128)S(1)}, u32[]{:S(2)}, u32[]{:S(2)}) %collective-permute-start.14) | collective-permute-done | bytes 524320 | tf_op jit(solution)/shard_map/ppermute | solution.py:14
  292.5 7.2 %convolution_bitcast_fusion.5 = f32[32,1024]{1,0:T(8,128)S(1)} fusion(f32[16,128,1024]{2,1,0:T(8,128)} %param.22, f32[16,32,128]{2,0,1:T(8,128)S(1)} %fusion.6), kind=kOutput, calls=%fused_computation.8 | convolution fusion | flops 805306368 | bytes 8781824 | tf_op jit(solution)/shard_map/ktp,krt->rp/dot_general | solution.py:130
  306.8 4.6 convolution_bitcast_fusion.4
  311.7 34.2 %all-reduce.16.cloned.1.call-done = f32[8,32,128]{2,1,0:T(8,128)} async-done(((f32[8,32,128]{2,1,0:T(8,128)}), f32[8,32,128]{2,1,0:T(8,128)}) %all-reduce.16.cloned.1.call-update) | async-done | bytes 131088 | tf_op jit(solution)/shard_map/psum | solution.py:137
  351.1 5.8 %collective-permute-done.18 = f32[16,32,128]{2,1,0:T(8,128)S(1)} collective-permute-done((f32[16,32,128]{2,1,0:T(8,128)S(1)}, f32[16,32,128]{2,1,0:T(8,128)S(1)}, u32[]{:S(2)}, u32[]{:S(2)}) %collective-permute-start.18) | collective-permute-done | bytes 262176 | tf_op jit(solution)/shard_map/ppermute | solution.py:14
  358.5 7.2 %convolution_bitcast_fusion.9 = f32[32,512]{1,0:T(8,128)S(1)} fusion(f32[32,128,512]{2,1,0:T(8,128)} %param.23, f32[32,32,128]{2,0,1:T(8,128)S(1)} %fusion.12, f32[32,32,128]{2,0,1:T(8,128)S(1)} %fusion.4), kind=kOutput, calls=%fused_computation.12 | convolution fusion | flops 805437440 | bytes 9502720 | tf_op jit(solution)/shard_map/ktp,krt->rp/dot_general | solution.py:130
  371.7 32.5 %all-reduce.18.cloned.1.call-done = f32[8,32,128]{2,1,0:T(8,128)} async-done(((f32[8,32,128]{2,1,0:T(8,128)}), f32[8,32,128]{2,1,0:T(8,128)}) %all-reduce.18.cloned.1.call-update) | async-done | bytes 131088 | tf_op jit(solution)/shard_map/psum | solution.py:137
  407.5 6.1 %fusion.1 = f32[32,256,1]{1,0,2:T(8,128)S(1)} fusion(f32[32,128,256]{2,1,0:T(8,128)} %param.24, f32[32,32,128]{2,0,1:T(8,128)S(1)} %fusion.24, f32[32,32,128]{2,0,1:T(8,128)S(1)} %fusion.10, f32[32,32,128]{2,0,1:T(8,128)} %fusion.2, f32[32,256,1]{1,0,2:T(8,128)S(1)} %fusion.90), kind=kOutput, calls=%fused_computation.16 | convolution fusion | flops 402923520 | bytes 5832704 | tf_op jit(solution)/shard_map/ktp,krt->rp/dot_general | solution.py:130
  415.3 34.6 %all-reduce.20.cloned.1.call-done = f32[8,32,128]{2,1,0:T(8,128)} async-done(((f32[8,32,128]{2,1,0:T(8,128)}), f32[8,32,128]{2,1,0:T(8,128)}) %all-reduce.20.cloned.1.call-update) | async-done | bytes 131088 | tf_op jit(solution)/shard_map/psum | solution.py:137
  (128 shorter events, 77.7 us)
Async XLA Ops:
  7.2 49.6 %all-reduce.8.cloned.1.call-start = ((), (), s32[]{:S(2)}) async-start(), calls=%async_computation | async-start | bytes 262144 | tf_op jit(solution)/shard_map/psum | solution.py:89
  16.9 2.1 collective-permute-start
  19.7 96.6 %all-reduce.10.cloned.1.call-start = ((), (), s32[]{:S(2)}) async-start(), calls=%async_computation.1 | async-start | bytes 262144 | tf_op jit(solution)/shard_map/psum | solution.py:89
  71.2 8.4 %collective-permute-start.2 = (f32[16,32,128]{2,0,1:T(8,128)S(1)}, f32[16,32,128]{2,0,1:T(8,128)S(1)}, u32[]{:S(2)}, u32[]{:S(2)}) collective-permute-start(f32[16,32,128]{2,0,1:T(8,128)S(1)} %slice_select_fusion.2), channel_id=1, source_target_pairs={{0,8},{4,12},{8,0},{12,4},{16,24},{20,28},{24,16},{28,20},{1,9},{5... | collective-permute-start | bytes 786440 | tf_op jit(solution)/shard_map/ppermute | solution.py:14
  79.7 1.4 collective-permute-start.3
  81.8 114.3 %all-reduce.12.cloned.1.call-start = ((), (), s32[]{:S(2)}) async-start(), calls=%async_computation.2 | async-start | bytes 262144 | tf_op jit(solution)/shard_map/psum | solution.py:89
  121.5 1.4 collective-permute-start.4
  122.9 5.6 %collective-permute-start.5 = (f32[32,1024]{1,0:T(8,128)S(1)}, f32[32,1024]{1,0:T(8,128)S(1)}, u32[]{:S(2)}, u32[]{:S(2)}) collective-permute-start(f32[32,1024]{1,0:T(8,128)S(1)} %add.142), channel_id=1, source_target_pairs={{0,8},{4,12},{8,0},{12,4},{16,24},{20,28},{24,16},{28,20},{1,9},{5... | collective-permute-start | bytes 393224 | tf_op jit(solution)/shard_map/ppermute | solution.py:14
  139.4 13.2 %collective-permute-start.6 = (f32[32,32,128]{2,0,1:T(8,128)S(1)}, f32[32,32,128]{2,0,1:T(8,128)S(1)}, u32[]{:S(2)}, u32[]{:S(2)}) collective-permute-start(f32[32,32,128]{2,0,1:T(8,128)S(1)} %slice_select_fusion), channel_id=1, source_target_pairs={{0,16},{4,20},{8,24},{12,28},{16,0},{20,4},{24,8},{28,12},{1,17},{... | collective-permute-start | bytes 1572872 | tf_op jit(solution)/shard_map/ppermute | solution.py:14
  152.8 6.7 %collective-permute-start.7 = (f32[16,32,128]{2,0,1:T(8,128)S(1)}, f32[16,32,128]{2,0,1:T(8,128)S(1)}, u32[]{:S(2)}, u32[]{:S(2)}) collective-permute-start(f32[16,32,128]{2,0,1:T(8,128)S(1)} %slice_select_fusion.1), channel_id=1, source_target_pairs={{0,8},{4,12},{8,0},{12,4},{16,24},{20,28},{24,16},{28,20},{1,9},{5... | collective-permute-start | bytes 786440 | tf_op jit(solution)/shard_map/ppermute | solution.py:14
  161.7 105.4 %all-reduce.14.cloned.1.call-start = ((), (), s32[]{:S(2)}) async-start(), calls=%async_computation.3 | async-start | bytes 262144 | tf_op jit(solution)/shard_map/psum | solution.py:137
  204.3 1.6 collective-permute-start.9
  205.9 8.4 %collective-permute-start.10 = (f32[32,2048]{1,0:T(8,128)S(1)}, f32[32,2048]{1,0:T(8,128)S(1)}, u32[]{:S(2)}, u32[]{:S(2)}) collective-permute-start(f32[32,2048]{1,0:T(8,128)S(1)} %add.148), channel_id=1, source_target_pairs={{0,8},{4,12},{8,0},{12,4},{16,24},{20,28},{24,16},{28,20},{1,9},{5... | collective-permute-start | bytes 786440 | tf_op jit(solution)/shard_map/ppermute | solution.py:14
  214.4 7.6 %collective-permute-start.11 = (f32[32,2048]{1,0:T(8,128)S(1)}, f32[32,2048]{1,0:T(8,128)S(1)}, u32[]{:S(2)}, u32[]{:S(2)}) collective-permute-start(f32[32,2048]{1,0:T(8,128)S(1)} %add.149), channel_id=1, source_target_pairs={{0,16},{4,20},{8,24},{12,28},{16,0},{20,4},{24,8},{28,12},{1,17},{... | collective-permute-start | bytes 786440 | tf_op jit(solution)/shard_map/ppermute | solution.py:14
  232.5 113.3 %all-reduce.16.cloned.1.call-start = ((), (), s32[]{:S(2)}) async-start(), calls=%async_computation.4 | async-start | bytes 262144 | tf_op jit(solution)/shard_map/psum | solution.py:137
  267.0 1.6 collective-permute-start.12
  269.6 8.4 %collective-permute-start.13 = (f32[16,32,128]{2,1,0:T(8,128)S(1)}, f32[16,32,128]{2,1,0:T(8,128)S(1)}, u32[]{:S(2)}, u32[]{:S(2)}) collective-permute-start(f32[16,32,128]{2,1,0:T(8,128)S(1)} %maximum_select_fusion.3), channel_id=1, source_target_pairs={{0,8},{4,12},{8,0},{12,4},{16,24},{20,28},{24,16},{28,20},{1,9},{5... | collective-permute-start | bytes 786440 | tf_op jit(solution)/shard_map/ppermute | solution.py:14
  278.1 13.2 %collective-permute-start.14 = (f32[32,32,128]{2,1,0:T(8,128)S(1)}, f32[32,32,128]{2,1,0:T(8,128)S(1)}, u32[]{:S(2)}, u32[]{:S(2)}) collective-permute-start(f32[32,32,128]{2,1,0:T(8,128)S(1)} %maximum_select_fusion.1), channel_id=1, source_target_pairs={{0,16},{4,20},{8,24},{12,28},{16,0},{20,4},{24,8},{28,12},{1,17},{... | collective-permute-start | bytes 1572872 | tf_op jit(solution)/shard_map/ppermute | solution.py:14
  301.1 5.6 %collective-permute-start.16 = (f32[32,1024]{1,0:T(8,128)S(1)}, f32[32,1024]{1,0:T(8,128)S(1)}, u32[]{:S(2)}, u32[]{:S(2)}) collective-permute-start(f32[32,1024]{1,0:T(8,128)S(1)} %add.151), channel_id=1, source_target_pairs={{0,8},{4,12},{8,0},{12,4},{16,24},{20,28},{24,16},{28,20},{1,9},{5... | collective-permute-start | bytes 393224 | tf_op jit(solution)/shard_map/ppermute | solution.py:14
  311.4 92.9 %all-reduce.18.cloned.1.call-start = ((), (), s32[]{:S(2)}) async-start(), calls=%async_computation.5 | async-start | bytes 262144 | tf_op jit(solution)/shard_map/psum | solution.py:137
  345.9 1.6 collective-permute-start.17
  348.5 8.4 %collective-permute-start.18 = (f32[16,32,128]{2,1,0:T(8,128)S(1)}, f32[16,32,128]{2,1,0:T(8,128)S(1)}, u32[]{:S(2)}, u32[]{:S(2)}) collective-permute-start(f32[16,32,128]{2,1,0:T(8,128)S(1)} %maximum_select_fusion.4), channel_id=1, source_target_pairs={{0,8},{4,12},{8,0},{12,4},{16,24},{20,28},{24,16},{28,20},{1,9},{5... | collective-permute-start | bytes 786440 | tf_op jit(solution)/shard_map/ppermute | solution.py:14
  369.8 80.2 %all-reduce.20.cloned.1.call-start = ((), (), s32[]{:S(2)}) async-start(), calls=%async_computation.6 | async-start | bytes 262144 | tf_op jit(solution)/shard_map/psum | solution.py:137
  404.2 1.8 collective-permute-start.20
  (16 other events, 528.5 us)
Sparse Core Ops, SparseCore 0:
  19.8 37.0 all-reduce.7
  81.9 34.3 all-reduce.9
  161.8 34.3 all-reduce.11
  232.7 34.3 all-reduce.13
  311.5 34.3 all-reduce.15
  369.9 34.3 all-reduce.17
  415.5 34.4 all-reduce.19
where the time goes:
time: 469 us; the launch traced here: 462 us
  waiting for transfers between devices  318 us (68%)
  matrix products  94.8 us (20%)
  starting transfers between devices  17.2 us (4%)
  between operations  15.1 us (3%)
  other arithmetic  11.5 us (2%)
  local copies, waits for them, and re-layouts  5.29 us (1%)
    psum x4, waiting for transfers between devices, body(): solutions[level_in_tree] = lax.psum(value_partial_sum, 'row')  136 us
    psum x3, waiting for transfers between devices, body(): arriving = lax.psum(arriving, 'row')  106 us
    ppermute x21, waiting for transfers between devices, swapped(): lax.ppermute(x, axis, [(i, i ^ 1 << stride) for i in range(lax.axis_size(...  76.5 us
    dot_general x3, matrix products, body(): jnp.einsum('ktp,rp->krt', update[level_in_tree], solved, precision=TOP_PR...  25.5 us
    dot_general x3, matrix products, body(): jnp.einsum('ktp,krt->rp', update[level_in_tree], gathered, precision=TOP_...  20.5 us
    dot_general x4, matrix products, body(): jnp.einsum('hay,zy->hza', inverse_factor[level_in_tree], fixed_update, pr...  19.6 us
    ppermute x21, starting transfers between devices, swapped(): lax.ppermute(x, axis, [(i, i ^ 1 << stride) for i in range(lax.axis_size(...  16.2 us
    dot_general x4, matrix products, body(): jnp.einsum('dkx,dek->ex', inverse_factor[level_in_tree], source_vector, p...  14.6 us
  transfers between devices with their start and end apart: 28, of which 26 were waited for; matrix products, arithmetic and copies ran while one was open for 2% of the time, Pallas kernels for 0%

commit v1 on v0

v1 whole, which is shorter than its diff:
```python
import functools

import jax
import jax.numpy as jnp
from jax import lax
from jax.experimental import pallas as pl
from jax.experimental.pallas import tpu as pltpu
from jax.sharding import PartitionSpec as P

LANES = 128
SUB = 8
MESH = pl.DeviceIdType.MESH
LEVELS = 4


def split(x):
    hi = x.astype(jnp.bfloat16)
    lo = (x - hi.astype(jnp.float32)).astype(jnp.bfloat16)
    return hi, lo


def kernel(cfg, *refs):
    L, R = cfg["L"], cfg["R"]
    nT = cfg["nT"]
    rhs = cfg["rhs"]
    TB = rhs // SUB
    cols = cfg["cols"]
    nb = cfg["nb"]
    base = cfg["base"]
    it = iter(refs)
    index_ref = next(it)
    src_hbm = [next(it) for _ in range(LEVELS)]
    inv_hbm = [next(it) for _ in range(LEVELS)]
    upd_hbm = [None] + [next(it) for _ in range(LEVELS - 1)]
    out_hbm = [next(it) for _ in range(LEVELS)]
    src = [next(it) for _ in range(LEVELS)]
    inv = [next(it) for _ in range(LEVELS)]
    upd = [None] + [next(it) for _ in range(LEVELS - 1)]
    c_buf = next(it)
    pend = next(it)
    stack = next(it)
    w_split = next(it)
    y_split = next(it)
    y_part = next(it)
    y_full = [next(it) for _ in range(LEVELS)]
    z_part = next(it)
    s_full = [None] + [next(it) for _ in range(LEVELS - 1)]
    load_sem = next(it)
    out_sem = next(it)
    phases = {}
    for name, _, _ in cfg["phases"]:
        phases[name] = next(it)
    send_sem = next(it)
    recv_sem = next(it)
    phase_at = {name: i for i, (name, _, _) in enumerate(cfg["phases"])}

    leaf = lax.axis_index("leaf")
    row = lax.axis_index("row")

    loads = {}
    at = 0
    for d in reversed(range(LEVELS)):
        for tag, a, b in (("s", src_hbm, src), ("i", inv_hbm, inv), ("u", upd_hbm, upd)):
            if a[d] is None:
                continue
            copy = pltpu.make_async_copy(a[d], b[d], load_sem.at[at])
            copy.start()
            loads[tag, d] = copy
            at += 1

    barrier = pltpu.get_barrier_semaphore()
    for k in range(1, L):
        pl.semaphore_signal(barrier, inc=1, device_id=((leaf + k) % L, row), device_id_type=MESH)
    for k in range(1, R):
        pl.semaphore_signal(barrier, inc=1, device_id=(leaf, (row + k) % R), device_id_type=MESH)
    pl.semaphore_wait(barrier, L + R - 2)

    def leaf_group(d):
        G = L >> d
        first = (leaf // G) * G
        me = leaf % G
        return G, me, lambda other: (first + other, row)

    row_group = (R, row, lambda other: (leaf, other))

    def tiles(ref, start, n):
        return ref.at[pl.ds(start, n)]

    def wait_all(name, ref, n):
        i = phase_at[name]
        whole = ref.at[pl.ds(0, n)]
        pltpu.make_async_copy(whole, whole, recv_sem.at[i]).wait()
        pltpu.make_async_copy(whole, whole, send_sem.at[i]).wait()

    def reduce_scatter(name, group, source, at0, n, target, to):
        G, me, who = group
        recv = phases[name]
        i = phase_at[name]
        for k in range(1, G):
            other = (me + k) % G
            pltpu.make_async_remote_copy(
                src_ref=tiles(source, at0 + other * n, n),
                dst_ref=tiles(recv, (k - 1) * n, n),
                send_sem=send_sem.at[i],
                recv_sem=recv_sem.at[i],
                device_id=who(other),
                device_id_type=MESH,
            ).start()
        if G > 1:
            wait_all(name, recv, (G - 1) * n)
        total = source[pl.ds(at0 + me * n, n)]
        for k in range(1, G):
            total = total + recv[pl.ds((k - 1) * n, n)]
        target[pl.ds(to, n)] = total

    def all_gather(name, group, full, n):
        G, me, who = group
        i = phase_at[name]
        for k in range(1, G):
            other = (me + k) % G
            pltpu.make_async_remote_copy(
                src_ref=tiles(full, me * n, n),
                dst_ref=tiles(full, me * n, n),
                send_sem=send_sem.at[i],
                recv_sem=recv_sem.at[i],
                device_id=who(other),
                device_id_type=MESH,
            ).start()
        if G > 1:
            wait_all(name, full, (G - 1) * n)

    def put_w(pair, half, block):
        hi, lo = split(block)
        w_split[pair, 0:rhs, half * LANES:(half + 1) * LANES] = hi
        w_split[pair, rhs:2 * rhs, half * LANES:(half + 1) * LANES] = lo

    def fill_y(values, d):
        for cb in range(cols[d] // LANES):
            hi, lo = split(values(cb))
            y_split[0:rhs, cb * LANES:(cb + 1) * LANES] = hi
            y_split[rhs:2 * rhs, cb * LANES:(cb + 1) * LANES] = lo

    def block_of(ref, b):
        return ref[pl.ds(b * TB, TB)].reshape(rhs, LANES)

    def over_rows(mat, rows, width, target):
        step = min(512, width)
        for nt in range(width // step):
            def body(k, acc):
                m = mat[pl.ds(k * 256, 256), nt * step:(nt + 1) * step]
                hi, lo = split(m)
                w = w_split[k]
                p = jnp.dot(w, hi, preferred_element_type=jnp.float32)
                q = jnp.dot(w[:rhs], lo, preferred_element_type=jnp.float32)
                return acc + (p[:rhs] + (p[rhs:] + q))
            acc = lax.fori_loop(0, rows // 256, body, jnp.zeros((rhs, step), jnp.float32), unroll=2 if rows >= 512 else 1)
            for c in range(step // LANES):
                target[pl.ds((nt * (step // LANES) + c) * TB, TB)] = acc[:, c * LANES:(c + 1) * LANES].reshape(TB, SUB, LANES)

    def over_cols(mat, rows, width, target):
        step = min(512, width)
        dims = (((1,), (1,)), ((), ()))

        def body(rt, carry):
            acc = jnp.zeros((rhs, 256), jnp.float32)
            for pc in range(width // step):
                m = mat[pl.ds(rt * 256, 256), pc * step:(pc + 1) * step]
                hi, lo = split(m)
                y = y_split[:, pc * step:(pc + 1) * step]
                p = lax.dot_general(y, hi, dims, preferred_element_type=jnp.float32)
                q = lax.dot_general(y[:rhs], lo, dims, preferred_element_type=jnp.float32)
                acc = acc + (p[:rhs] + (p[rhs:] + q))
            target[pl.ds(rt * 2 * TB, TB)] = acc[:, :LANES].reshape(TB, SUB, LANES)
            target[pl.ds(rt * 2 * TB + TB, TB)] = acc[:, LANES:].reshape(TB, SUB, LANES)
            return carry

        lax.fori_loop(0, rows // 256, body, 0, unroll=2 if rows >= 512 else 1)

    own_blocks = nT // TB
    zn = nT // R
    for d in reversed(range(LEVELS)):
        group = leaf_group(d)
        G, me, _ = group
        loads["s", d].wait()
        if d < LEVELS - 1:
            reduce_scatter(f"pend{d}", group, pend, base[d], nT, z_part, 0)
            full = phases[f"wg{d}"]
            reduce_scatter(f"wr{d}", row_group, z_part, 0, zn, full, row * zn)
            all_gather(f"wg{d}", row_group, full, zn)
        for b in range(own_blocks):
            w = block_of(src[d], b)
            if d < LEVELS - 1:
                w = w - block_of(full, b)
            put_w(b // 2, b % 2, w)
        loads["i", d].wait()
        yn = cols[d] // LANES * TB // G
        if G > 1:
            over_rows(inv[d], nT // TB * LANES, cols[d], y_part)
            reduce_scatter(f"yr{d}", group, y_part, 0, yn, y_full[d], me * yn)
            all_gather(f"yg{d}", group, y_full[d], yn)
        else:
            over_rows(inv[d], nT // TB * LANES, cols[d], y_full[d])
        fill_y(lambda cb: block_of(y_full[d], cb), d)
        if d > 0:
            loads["u", d].wait()
            over_cols(upd[d], nb[d] * LANES, cols[d], c_buf)
            c_buf[pl.ds(nb[d] * TB, TB)] = jnp.zeros((TB, SUB, LANES), jnp.float32)
            first = cfg["inv_at"][d]

            def scatter(b, carry):
                j = index_ref[first + b]
                term = c_buf[pl.ds(j * TB, TB)]
                where = pl.ds(b * TB, TB)
                if d < LEVELS - 1:
                    term = pend[where] + term
                pend[where] = term
                return carry

            lax.fori_loop(0, base[d] // TB, scatter, 0, unroll=2)

    finals = []
    for d in range(LEVELS):
        group = leaf_group(d)
        G, me, _ = group
        if d > 0:
            first = cfg["idx_at"][d]

            def gather(pair, carry):
                for half in range(2):
                    b = index_ref[first + pair * 2 + half]
                    put_w(pair, half, stack[pl.ds(b * TB, TB)].reshape(rhs, LANES))
                return carry

            lax.fori_loop(0, nb[d] // 2, gather, 0, unroll=2)
            yn = cols[d] // LANES * TB // G
            if G > 1:
                over_rows(upd[d], nb[d] * LANES, cols[d], y_part)
                reduce_scatter(f"sr{d}", group, y_part, 0, yn, s_full[d], me * yn)
                all_gather(f"sg{d}", group, s_full[d], yn)
            else:
                over_rows(upd[d], nb[d] * LANES, cols[d], s_full[d])
            fill_y(lambda cb: block_of(y_full[d], cb) - block_of(s_full[d], cb), d)
        over_cols(inv[d], nT // TB * LANES, cols[d], z_part)
        full = phases[f"ag{d}"]
        reduce_scatter(f"ar{d}", row_group, z_part, 0, zn, full, row * zn)
        all_gather(f"ag{d}", row_group, full, zn)
        final = pltpu.make_async_copy(full, out_hbm[d], out_sem.at[d])
        final.start()
        finals.append(final)
        if d < LEVELS - 1:
            front = phases[f"fg{d}"]
            front[pl.ds(me * nT, nT)] = full[...]
            all_gather(f"fg{d}", group, front, nT)
            stack[pl.ds(base[d], G * nT)] = front[...]
    for final in finals:
        final.wait()


def make_body(L, R):
    def body(*args):
        sources, inverse, update, links = args[0:4], args[4:8], (None,) + args[8:11], (None,) + args[11:14]
        own, rhs, lanes = sources[0].shape
        TB = rhs // SUB
        nT = own * TB
        blocks = own * L
        counts = [blocks >> d for d in range(LEVELS)]
        bases = [sum(counts[:d]) for d in range(LEVELS)]
        cols = [a.shape[2] for a in inverse]
        nb = [0] + [a.shape[0] for a in update[1:]]

        pieces = []
        idx_at, inv_at = [0] * LEVELS, [0] * LEVELS
        at = 0
        for d in range(1, LEVELS):
            link = links[d].astype(jnp.int32)
            level = link // blocks
            idx = jnp.zeros_like(link)
            for u in range(d):
                idx = jnp.where(level == u, bases[u] + link % counts[u], idx)
            idx_at[d] = at
            at += nb[d]
            number = jnp.arange(nb[d], dtype=jnp.int32)
            hits = idx[:, None] == jnp.arange(bases[d], dtype=jnp.int32)[None, :]
            inverse_map = nb[d] + jnp.sum(jnp.where(hits, (number - nb[d])[:, None], 0), axis=0)
            inv_at[d] = at
            at += bases[d]
            pieces += [idx, inverse_map.astype(jnp.int32)]
        index = jnp.concatenate(pieces)

        tile = lambda n: (n, SUB, LANES)
        phases = []
        for d in range(LEVELS):
            G = L >> d
            yt = cols[d] // LANES * TB
            if d < LEVELS - 1:
                phases.append((f"pend{d}", (G - 1) * nT, True))
                phases.append((f"wr{d}", (R - 1) * (nT // R), True))
                phases.append((f"wg{d}", nT, True))
                phases.append((f"fg{d}", G * nT, True))
            if G > 1:
                phases.append((f"yr{d}", (G - 1) * (yt // G), True))
                phases.append((f"yg{d}", 1, False))
                if d > 0:
                    phases.append((f"sr{d}", (G - 1) * (yt // G), True))
                    phases.append((f"sg{d}", 1, False))
            phases.append((f"ar{d}", (R - 1) * (nT // R), True))
            phases.append((f"ag{d}", nT, True))
        cfg = dict(
            L=L, R=R, nT=nT, rhs=rhs, cols=cols, nb=nb, base=[b * TB for b in bases],
            idx_at=idx_at, inv_at=inv_at, phases=phases,
        )
        f32 = jnp.float32
        max_cols = max(cols)
        max_rows = max(max(nb), own)
        scratch = []
        scratch += [pltpu.VMEM(tile(nT), f32) for _ in range(LEVELS)]
        scratch += [pltpu.VMEM((a.shape[0] * a.shape[1], a.shape[2]), f32) for a in inverse]
        scratch += [pltpu.VMEM((a.shape[0] * a.shape[1], a.shape[2]), f32) for a in update[1:]]
        scratch.append(pltpu.VMEM(tile((max(nb) + 1) * TB), f32))
        scratch.append(pltpu.VMEM(tile(bases[-1] * TB), f32))
        scratch.append(pltpu.VMEM(tile(bases[-1] * TB), f32))
        scratch.append(pltpu.VMEM((max_rows // 2, 2 * rhs, 2 * LANES), jnp.bfloat16))
        scratch.append(pltpu.VMEM((2 * rhs, max_cols), jnp.bfloat16))
        scratch.append(pltpu.VMEM(tile(max_cols // LANES * TB), f32))
        scratch += [pltpu.VMEM(tile(cols[d] // LANES * TB), f32) for d in range(LEVELS)]
        scratch.append(pltpu.VMEM(tile(nT), f32))
        scratch += [pltpu.VMEM(tile(cols[d] // LANES * TB), f32) for d in range(1, LEVELS)]
        scratch.append(pltpu.SemaphoreType.DMA((3 * LEVELS,)))
        scratch.append(pltpu.SemaphoreType.DMA((LEVELS,)))
        scratch += [pltpu.VMEM(tile(n), f32) for _, n, _ in phases]
        scratch.append(pltpu.SemaphoreType.DMA((len(phases),)))
        scratch.append(pltpu.SemaphoreType.DMA((len(phases),)))

        operands = [index]
        operands += [a.reshape(tile(nT)) for a in sources]
        operands += [a.reshape(-1, a.shape[2]) for a in inverse]
        operands += [a.reshape(-1, a.shape[2]) for a in update[1:]]
        anywhere = pl.BlockSpec(memory_space=pl.ANY)
        outs = pl.pallas_call(
            functools.partial(kernel, cfg),
            name="solve",
            out_shape=[jax.ShapeDtypeStruct(tile(nT), f32)] * LEVELS,
            in_specs=[pl.BlockSpec(memory_space=pltpu.SMEM)] + [anywhere] * (len(operands) - 1),
            out_specs=[anywhere] * LEVELS,
            scratch_shapes=scratch,
            compiler_params=pltpu.CompilerParams(
                collective_id=0, has_side_effects=True, vmem_limit_bytes=67043328 - (1 << 20)
            ),
        )(*operands)
        return tuple(o.reshape(own, rhs, lanes) for o in outs)

    return body


def solution(mesh):
    rows = P("leaf", None, None)
    factor = P("leaf", None, "row")
    return jax.shard_map(
        make_body(mesh.shape["leaf"], mesh.shape["row"]),
        mesh=mesh,
        in_specs=(rows,) * 4 + (factor,) * 7 + (P("leaf"),) * 3,
        out_specs=(rows,) * 4,
        check_vma=False,
    )
```

time: 469 us -> 172 us (0.37); the launches traced: 462 us -> 172 us
  waiting for transfers between devices: 318 us -> 0 us
  Pallas kernels: 0 us -> 162 us
  matrix products: 94.8 us -> 0 us
  starting transfers between devices: 17.2 us -> 0 us
  between operations: 15.1 us -> 0.66 us
  other arithmetic: 11.5 us -> 2.29 us
    psum x7 -> x0, waiting for transfers between devices: 241 us -> none  [the longest x4 136 us: body(): solutions[level_in_tree] = lax.psum(value_partial_sum, 'row')]
    pallas_call x0 -> x1, Pallas kernels: none -> 162 us  [body(): pl.pallas_call(functools.partial(kernel, cfg), name='solve', out_shape=[j...]
    dot_general x26 -> x0, matrix products: 94.8 us -> none  [the longest x3 25.5 us: body(): jnp.einsum('ktp,rp->krt', update[level_in_tree], solved, precision=TOP_PR...]
    ppermute x21 -> x0, waiting for transfers between devices: 76.5 us -> none  [swapped(): lax.ppermute(x, axis, [(i, i ^ 1 << stride) for i in range(lax.axis_size(...]
    ppermute x21 -> x0, starting transfers between devices: 16.2 us -> none  [swapped(): lax.ppermute(x, axis, [(i, i ^ 1 << stride) for i in range(lax.axis_size(...]
  transfers between devices with their start and end apart: 28 -> 0, of which waited for: 26 -> 0; matrix products, arithmetic and copies ran while one was open for 2% -> 0% of each run, Pallas kernels for 0% -> 0%
where the time goes in v1:
time: 172 us
  Pallas kernels  162 us (94%)
  local copies, waits for them, and re-layouts  6.93 us (4%)
  other arithmetic  2.29 us (1%)
    pallas_call x1, Pallas kernels, body(): pl.pallas_call(functools.partial(kernel, cfg), name='solve', out_shape=[j...  162 us
    unnamed x4, local copies, waits for them, and re-layouts  6.27 us

profile of v1, /device:TPU:0, one launch (start us, length us, event | category | flops | bytes accessed | tf_op | source)
XLA Modules:
  0.0 171.9 jit_solution(15502431761859973284)
XLA Ops:
  0.6 0.7 compare_select_fusion.2
  1.3 0.7 compare_select_fusion.5
  2.0 0.1 select_reduce_fusion.2
  2.1 0.7 compare_select_fusion.4
  2.7 0.1 select_reduce_fusion.1
  2.8 0.1 select_reduce_fusion
  2.9 0.7 concatenate.3.refs_0_
  3.6 162.0 %solve.1 = (f32[32,8,128]{2,1,0:T(8,128)}, f32[32,8,128]{2,1,0:T(8,128)}, f32[32,8,128]{2,1,0:T(8,128)}, f32[32,8,128]{2,1,0:T(8,128)}) custom-call(s32[352]{0:T(512)} %concatenate.3.refs_0_, f32[32,8,128]{2,1,0:T(8,128)} %bitcast.22, f32[32,8,128]{2,1,0:T(8,128)} %bitcast.23, f32[32,8,128]{2,1,0:T(8,128)} %bitcast.24, f32[32,8,128]{2,1,0:T(8,128)} %bitcast.25, ...), custom_call_target="tpu_custom_call" | custom-call | tf_op jit(solution)/shard_map/solve/pallas_call | solution.py:339
  165.6 1.6 copy.22
  167.2 1.6 copy.23
  168.8 1.6 copy.24
  170.3 1.6 copy.25
  (3 shorter events, 0.0 us)

commit v2 on v1

--- a/solution.py
+++ b/solution.py
@@ -48,11 +48,9 @@
     load_sem = next(it)
     out_sem = next(it)
     phases = {}
-    for name, _, _ in cfg["phases"]:
+    for name, _ in cfg["phases"]:
         phases[name] = next(it)
-    send_sem = next(it)
-    recv_sem = next(it)
-    phase_at = {name: i for i, (name, _, _) in enumerate(cfg["phases"])}
+    sems = next(it)
 
     leaf = lax.axis_index("leaf")
     row = lax.axis_index("row")
@@ -81,53 +79,178 @@
         me = leaf % G
         return G, me, lambda other: (first + other, row)
 
-    row_group = (R, row, lambda other: (leaf, other))
-
     def tiles(ref, start, n):
         return ref.at[pl.ds(start, n)]
 
-    def wait_all(name, ref, n):
-        i = phase_at[name]
+    counter = [0]
+
+    def new_sem():
+        counter[0] += 1
+        return sems.at[counter[0] - 1]
+
+    def wait_tiles(sem, ref, n):
         whole = ref.at[pl.ds(0, n)]
-        pltpu.make_async_copy(whole, whole, recv_sem.at[i]).wait()
-        pltpu.make_async_copy(whole, whole, send_sem.at[i]).wait()
-
-    def reduce_scatter(name, group, source, at0, n, target, to):
+        pltpu.make_async_copy(whole, whole, sem).wait()
+
+    def push(source, target, out_s, in_s, device):
+        pltpu.make_async_remote_copy(
+            src_ref=source,
+            dst_ref=target,
+            send_sem=out_s,
+            recv_sem=in_s,
+            device_id=device,
+            device_id_type=MESH,
+        ).start()
+
+    def group_sum(name, group, source, total_tiles, target):
         G, me, who = group
         recv = phases[name]
-        i = phase_at[name]
+        if G == 2:
+            out_s, in_s = new_sem(), new_sem()
+            push(tiles(source, 0, total_tiles), tiles(recv, 0, total_tiles), out_s, in_s, who(1 - me))
+            wait_tiles(in_s, recv, total_tiles)
+            target[...] = source[pl.ds(0, total_tiles)] + recv[...]
+            wait_tiles(out_s, recv, total_tiles)
+            return
+        n = total_tiles // G
+        out_s, in_s = new_sem(), new_sem()
         for k in range(1, G):
             other = (me + k) % G
-            pltpu.make_async_remote_copy(
-                src_ref=tiles(source, at0 + other * n, n),
-                dst_ref=tiles(recv, (k - 1) * n, n),
-                send_sem=send_sem.at[i],
-                recv_sem=recv_sem.at[i],
-                device_id=who(other),
-                device_id_type=MESH,
-            ).start()
-        if G > 1:
-            wait_all(name, recv, (G - 1) * n)
-        total = source[pl.ds(at0 + me * n, n)]
+            push(tiles(source, other * n, n), tiles(recv, (k - 1) * n, n), out_s, in_s, who(other))
+        wait_tiles(in_s, recv, (G - 1) * n)
+        total = source[pl.ds(me * n, n)]
         for k in range(1, G):
             total = total + recv[pl.ds((k - 1) * n, n)]
-        target[pl.ds(to, n)] = total
-
-    def all_gather(name, group, full, n):
+        target[pl.ds(me * n, n)] = total
+        wait_tiles(out_s, recv, (G - 1) * n)
+        out_s, in_s = new_sem(), new_sem()
+        for k in range(1, G):
+            mine = tiles(target, me * n, n)
+            push(mine, mine, out_s, in_s, who((me + k) % G))
+        wait_tiles(in_s, target, (G - 1) * n)
+        wait_tiles(out_s, target, (G - 1) * n)
+
+    C, cn = cfg["C"], nT // cfg["C"]
+    half_row = R // 2
+    right = row // half_row
+    inward = row + 1 - 2 * right
+    outward = row - 1 + 2 * right
+    depth = (half_row - 1 - row) * (1 - right) + (row - half_row) * right
+
+    def row_sum(name, prepare, done):
+        came, across, full = phases[name + "i"], phases[name + "x"], phases[name + "f"]
+        out_in, out_back = new_sem(), new_sem()
+        in_s = [new_sem() for _ in range(C)]
+        x_s = [new_sem() for _ in range(C)]
+        f_s = [new_sem() for _ in range(C)]
+        for c in range(C):
+            part = tiles(z_part, c * cn, cn)
+            prepare(c)
+            if half_row > 1:
+                @pl.when(depth < half_row - 1)
+                def _():
+                    wait_tiles(in_s[c], came, cn)
+                    z_part[pl.ds(c * cn, cn)] = z_part[pl.ds(c * cn, cn)] + came[pl.ds(c * cn, cn)]
+
+                @pl.when(depth > 0)
+                def _():
+                    push(part, tiles(came, c * cn, cn), out_in, in_s[c], (leaf, inward))
+
+            @pl.when(depth == 0)
+            def _():
+                push(part, tiles(across, c * cn, cn), out_in, x_s[c], (leaf, inward))
+        for c in range(C):
+            here = tiles(full, c * cn, cn)
+
+            @pl.when(depth == 0)
+            def _():
+                wait_tiles(x_s[c], across, cn)
+                full[pl.ds(c * cn, cn)] = z_part[pl.ds(c * cn, cn)] + across[pl.ds(c * cn, cn)]
+
+            if half_row > 1:
+                @pl.when(depth > 0)
+                def _():
+                    wait_tiles(f_s[c], full, cn)
+
+                @pl.when(depth < half_row - 1)
+                def _():
+                    push(here, here, out_back, f_s[c], (leaf, outward))
+            done(c, full)
+
+        def finish():
+            wait_tiles(out_in, full, nT)
+            if half_row > 1:
+                @pl.when(depth < half_row - 1)
+                def _():
+                    wait_tiles(out_back, full, nT)
+
+        return full, finish
+
+    def pend_scatter(d, group):
         G, me, who = group
-        i = phase_at[name]
-        for k in range(1, G):
-            other = (me + k) % G
-            pltpu.make_async_remote_copy(
-                src_ref=tiles(full, me * n, n),
-                dst_ref=tiles(full, me * n, n),
-                send_sem=send_sem.at[i],
-                recv_sem=recv_sem.at[i],
-                device_id=who(other),
-                device_id_type=MESH,
-            ).start()
-        if G > 1:
-            wait_all(name, full, (G - 1) * n)
+        H, chip, core = G // 2, me // 2, me % 2
+        from_core, from_chip = phases[f"pc{d}"], phases[f"ph{d}"]
+        out_core, out_chip = new_sem(), new_sem()
+        core_s = [new_sem() for _ in range(H)]
+        chip_s = [new_sem() for _ in range(C)]
+        for k in list(range(1, H)) + [0]:
+            ch = (chip + k) % H
+            push(tiles(pend, base[d] + (2 * ch + 1 - core) * nT, nT), tiles(from_core, k * nT, nT), out_core, core_s[k], who(2 * chip + 1 - core))
+        for c in range(C):
+            for k in range(1, H):
+                ch = (chip + k) % H
+                if c == 0:
+                    wait_tiles(core_s[k], from_core, nT)
+                where = pl.ds(base[d] + (2 * ch + core) * nT + c * cn, cn)
+                pend[where] = pend[where] + from_core[pl.ds(k * nT + c * cn, cn)]
+                push(pend.at[where], tiles(from_chip, (k - 1) * nT + c * cn, cn), out_chip, chip_s[c], who(2 * ch + core))
+
+        def prepare(c):
+            if c == 0:
+                wait_tiles(core_s[0], from_core, nT)
+            total = pend[pl.ds(base[d] + me * nT + c * cn, cn)] + from_core[pl.ds(c * cn, cn)]
+            if H > 1:
+                wait_tiles(chip_s[c], from_chip, (H - 1) * cn)
+            for k in range(1, H):
+                total = total + from_chip[pl.ds((k - 1) * nT + c * cn, cn)]
+            z_part[pl.ds(c * cn, cn)] = total
+
+        def finish():
+            wait_tiles(out_core, pend, H * nT)
+            if H > 1:
+                wait_tiles(out_chip, pend, (H - 1) * nT)
+
+        return prepare, finish
+
+    def front_gather(d, group):
+        G, me, who = group
+        H, chip, core = G // 2, me // 2, me % 2
+        front = phases[f"fg{d}"]
+        out_s, core_s = new_sem(), new_sem()
+        chip_s = [new_sem() for _ in range(C)]
+        partner = who(2 * chip + 1 - core)
+
+        def done(c, full):
+            mine = tiles(full, c * cn, cn)
+            target = tiles(front, me * nT + c * cn, cn)
+            for k in range(1, H):
+                push(mine, target, out_s, chip_s[c], who(2 * ((chip + k) % H) + core))
+            push(mine, target, out_s, core_s, partner)
+            front[pl.ds(me * nT + c * cn, cn)] = full[pl.ds(c * cn, cn)]
+
+        def finish():
+            for c in range(C):
+                if H > 1:
+                    wait_tiles(chip_s[c], front, (H - 1) * cn)
+                for k in range(1, H):
+                    other = 2 * ((chip + k) % H) + core
+                    piece = tiles(front, other * nT + c * cn, cn)
+                    push(piece, piece, out_s, core_s, partner)
+            wait_tiles(core_s, front, H * nT)
+            wait_tiles(out_s, front, (2 * H - 1) * nT)
+            stack[pl.ds(base[d], G * nT)] = front[...]
+
+        return done, finish
 
     def put_w(pair, half, block):
         hi, lo = split(block)
@@ -157,7 +280,7 @@
             for c in range(step // LANES):
                 target[pl.ds((nt * (step // LANES) + c) * TB, TB)] = acc[:, c * LANES:(c + 1) * LANES].reshape(TB, SUB, LANES)
 
-    def over_cols(mat, rows, width, target):
+    def over_cols(mat, rows, width, target, chunk=None):
         step = min(512, width)
         dims = (((1,), (1,)), ((), ()))
 
@@ -174,30 +297,33 @@
             target[pl.ds(rt * 2 * TB + TB, TB)] = acc[:, LANES:].reshape(TB, SUB, LANES)
             return carry
 
-        lax.fori_loop(0, rows // 256, body, 0, unroll=2 if rows >= 512 else 1)
-
-    own_blocks = nT // TB
-    zn = nT // R
+        if chunk is not None:
+            body(chunk, 0)
+        else:
+            lax.fori_loop(0, rows // 256, body, 0, unroll=2 if rows >= 512 else 1)
+
     for d in reversed(range(LEVELS)):
         group = leaf_group(d)
         G, me, _ = group
         loads["s", d].wait()
         if d < LEVELS - 1:
-            reduce_scatter(f"pend{d}", group, pend, base[d], nT, z_part, 0)
-            full = phases[f"wg{d}"]
-            reduce_scatter(f"wr{d}", row_group, z_part, 0, zn, full, row * zn)
-            all_gather(f"wg{d}", row_group, full, zn)
-        for b in range(own_blocks):
-            w = block_of(src[d], b)
-            if d < LEVELS - 1:
-                w = w - block_of(full, b)
-            put_w(b // 2, b % 2, w)
+            prepare, sent = pend_scatter(d, group)
+
+            def done(c, full):
+                for half in range(2):
+                    b = 2 * c + half
+                    put_w(c, half, block_of(src[d], b) - block_of(full, b))
+
+            _, finish = row_sum(f"w{d}", prepare, done)
+            finish()
+            sent()
+        else:
+            for b in range(nT // TB):
+                put_w(b // 2, b % 2, block_of(src[d], b))
         loads["i", d].wait()
-        yn = cols[d] // LANES * TB // G
         if G > 1:
             over_rows(inv[d], nT // TB * LANES, cols[d], y_part)
-            reduce_scatter(f"yr{d}", group, y_part, 0, yn, y_full[d], me * yn)
-            all_gather(f"yg{d}", group, y_full[d], yn)
+            group_sum(f"y{d}", group, y_part, cols[d] // LANES * TB, y_full[d])
         else:
             over_rows(inv[d], nT // TB * LANES, cols[d], y_full[d])
         fill_y(lambda cb: block_of(y_full[d], cb), d)
@@ -232,28 +358,32 @@
                 return carry
 
             lax.fori_loop(0, nb[d] // 2, gather, 0, unroll=2)
-            yn = cols[d] // LANES * TB // G
             if G > 1:
                 over_rows(upd[d], nb[d] * LANES, cols[d], y_part)
-                reduce_scatter(f"sr{d}", group, y_part, 0, yn, s_full[d], me * yn)
-                all_gather(f"sg{d}", group, s_full[d], yn)
+                group_sum(f"s{d}", group, y_part, cols[d] // LANES * TB, s_full[d])
             else:
                 over_rows(upd[d], nb[d] * LANES, cols[d], s_full[d])
             fill_y(lambda cb: block_of(y_full[d], cb) - block_of(s_full[d], cb), d)
-        over_cols(inv[d], nT // TB * LANES, cols[d], z_part)
-        full = phases[f"ag{d}"]
-        reduce_scatter(f"ar{d}", row_group, z_part, 0, zn, full, row * zn)
-        all_gather(f"ag{d}", row_group, full, zn)
+        if d < LEVELS - 1:
+            done, gathered = front_gather(d, group)
+        else:
+            done = lambda c, full: None
+        full, finish = row_sum(
+            f"a{d}", lambda c: over_cols(inv[d], nT // TB * LANES, cols[d], z_part, c), done
+        )
         final = pltpu.make_async_copy(full, out_hbm[d], out_sem.at[d])
         final.start()
         finals.append(final)
         if d < LEVELS - 1:
-            front = phases[f"fg{d}"]
-            front[pl.ds(me * nT, nT)] = full[...]
-            all_gather(f"fg{d}", group, front, nT)
-            stack[pl.ds(base[d], G * nT)] = front[...]
+            gathered()
+        finish()
     for final in finals:
         final.wait()
+
+
+def hand_over(*refs):
+    for d in range(LEVELS):
+        refs[LEVELS + d][...] = refs[d][...]
 
 
 def make_body(L, R):
@@ -289,25 +419,31 @@
 
         tile = lambda n: (n, SUB, LANES)
         phases = []
+        C = max(1, own // 2)
+        n_sems = 0
         for d in range(LEVELS):
             G = L >> d
             yt = cols[d] // LANES * TB
+            kinds = ["a"]
             if d < LEVELS - 1:
-                phases.append((f"pend{d}", (G - 1) * nT, True))
-                phases.append((f"wr{d}", (R - 1) * (nT // R), True))
-                phases.append((f"wg{d}", nT, True))
-                phases.append((f"fg{d}", G * nT, True))
+                kinds.append("w")
+                phases.append((f"pc{d}", G // 2 * nT))
+                phases.append((f"ph{d}", max(1, (G // 2 - 1) * nT)))
+                phases.append((f"fg{d}", G * nT))
+                n_sems += 2 + G // 2 + C + 2 + C
+            for kind in kinds:
+                phases += [(kind + str(d) + part, nT) for part in "ixf"]
+                n_sems += 2 + 3 * C
             if G > 1:
-                phases.append((f"yr{d}", (G - 1) * (yt // G), True))
-                phases.append((f"yg{d}", 1, False))
+                n = yt if G == 2 else (G - 1) * (yt // G)
+                phases.append((f"y{d}", n))
+                n_sems += 4
                 if d > 0:
-                    phases.append((f"sr{d}", (G - 1) * (yt // G), True))
-                    phases.append((f"sg{d}", 1, False))
-            phases.append((f"ar{d}", (R - 1) * (nT // R), True))
-            phases.append((f"ag{d}", nT, True))
+                    phases.append((f"s{d}", n))
+                    n_sems += 4
         cfg = dict(
             L=L, R=R, nT=nT, rhs=rhs, cols=cols, nb=nb, base=[b * TB for b in bases],
-            idx_at=idx_at, inv_at=inv_at, phases=phases,
+            idx_at=idx_at, inv_at=inv_at, phases=phases, C=C,
         )
         f32 = jnp.float32
         max_cols = max(cols)
@@ -327,9 +463,8 @@
         scratch += [pltpu.VMEM(tile(cols[d] // LANES * TB), f32) for d in range(1, LEVELS)]
         scratch.append(pltpu.SemaphoreType.DMA((3 * LEVELS,)))
         scratch.append(pltpu.SemaphoreType.DMA((LEVELS,)))
-        scratch += [pltpu.VMEM(tile(n), f32) for _, n, _ in phases]
-        scratch.append(pltpu.SemaphoreType.DMA((len(phases),)))
-        scratch.append(pltpu.SemaphoreType.DMA((len(phases),)))
+        scratch += [pltpu.VMEM(tile(n), f32) for _, n in phases]
+        scratch.append(pltpu.SemaphoreType.DMA((n_sems,)))
 
         operands = [index]
         operands += [a.reshape(tile(nT)) for a in sources]
@@ -347,6 +482,13 @@
                 collective_id=0, has_side_effects=True, vmem_limit_bytes=67043328 - (1 << 20)
             ),
         )(*operands)
+        outs = pl.pallas_call(
+            hand_over,
+            name="hand_over",
+            out_shape=[jax.ShapeDtypeStruct(tile(nT), f32)] * LEVELS,
+            in_specs=[pl.BlockSpec(memory_space=pltpu.VMEM)] * LEVELS,
+            out_specs=[pl.BlockSpec(memory_space=pltpu.VMEM)] * LEVELS,
+        )(*outs)
         return tuple(o.reshape(own, rhs, lanes) for o in outs)
 
     return body

time: 172 us -> 160 us (0.930)
  local copies, waits for them, and re-layouts: 6.93 us -> 0.67 us
  Pallas kernels: 162 us -> 156 us
    pallas_call x1, Pallas kernels: 162 us -> 154 us  [body(): pl.pallas_call(functools.partial(kernel, cfg), name='solve', out_shape=[j...]
    unnamed x4 -> x0, local copies, waits for them, and re-layouts: 6.27 us -> none
    pallas_call x0 -> x1, Pallas kernels: none -> 1.89 us  [body(): pl.pallas_call(hand_over, name='hand_over', out_shape=[jax.ShapeDtypeStru...]
where the time goes in v2:
time: 160 us
  Pallas kernels  156 us (98%)
  other arithmetic  2.29 us (1%)
    pallas_call x1, Pallas kernels, body(): pl.pallas_call(functools.partial(kernel, cfg), name='solve', out_shape=[j...  154 us

profile of v2, /device:TPU:0, one launch (start us, length us, event | category | flops | bytes accessed | tf_op | source)
XLA Modules:
  0.0 159.8 jit_solution(10190560965859249195)
XLA Ops:
  0.6 0.7 compare_select_fusion.2
  1.3 0.7 compare_select_fusion.5
  2.0 0.1 select_reduce_fusion.2
  2.1 0.7 compare_select_fusion.4
  2.7 0.1 select_reduce_fusion.1
  2.8 0.1 select_reduce_fusion
  2.9 0.7 concatenate.3.refs_0_
  3.6 154.3 %solve.1 = (f32[32,8,128]{2,1,0:T(8,128)}, f32[32,8,128]{2,1,0:T(8,128)}, f32[32,8,128]{2,1,0:T(8,128)}, f32[32,8,128]{2,1,0:T(8,128)}) custom-call(s32[352]{0:T(512)} %concatenate.3.refs_0_, f32[32,8,128]{2,1,0:T(8,128)} %bitcast.22, f32[32,8,128]{2,1,0:T(8,128)} %bitcast.23, f32[32,8,128]{2,1,0:T(8,128)} %bitcast.24, f32[32,8,128]{2,1,0:T(8,128)} %bitcast.25, ...), custom_call_target="tpu_custom_call" | custom-call | tf_op jit(solution)/shard_map/solve/pallas_call | solution.py:474
  157.9 1.9 %hand_over.1 = (f32[32,8,128]{2,1,0:T(8,128)}, f32[32,8,128]{2,1,0:T(8,128)}, f32[32,8,128]{2,1,0:T(8,128)}, f32[32,8,128]{2,1,0:T(8,128)}) custom-call(f32[32,8,128]{2,1,0:T(8,128)} %get-tuple-element.12.refs_0_, f32[32,8,128]{2,1,0:T(8,128)} %get-tuple-element.13.refs_1_, f32[32,8,128]{2,1,0:T(8,128)} %get-tuple-element.14.refs_2_, ...), custom_call_target="tpu_custom_call" | custom-call | tf_op jit(solution)/shard_map/hand_over/pallas_call | solution.py:485
  (3 shorter events, 0.0 us)

commit v3 on v2

--- a/solution.py
+++ b/solution.py
@@ -102,10 +102,11 @@
             device_id_type=MESH,
         ).start()
 
-    def group_sum(name, group, source, total_tiles, target):
+    def group_sum(name, group, source, total_tiles, target, compute):
         G, me, who = group
         recv = phases[name]
         if G == 2:
+            compute(None)
             out_s, in_s = new_sem(), new_sem()
             push(tiles(source, 0, total_tiles), tiles(recv, 0, total_tiles), out_s, in_s, who(1 - me))
             wait_tiles(in_s, recv, total_tiles)
@@ -114,9 +115,15 @@
             return
         n = total_tiles // G
         out_s, in_s = new_sem(), new_sem()
-        for k in range(1, G):
-            other = (me + k) % G
-            push(tiles(source, other * n, n), tiles(recv, (k - 1) * n, n), out_s, in_s, who(other))
+
+        def ready(start, stop):
+            for other in range(start // n, stop // n):
+                @pl.when(me != other)
+                def _():
+                    slot = (other - me + G) % G - 1
+                    push(tiles(source, other * n, n), tiles(recv, slot * n, n), out_s, in_s, who(other))
+
+        compute(ready)
         wait_tiles(in_s, recv, (G - 1) * n)
         total = source[pl.ds(me * n, n)]
         for k in range(1, G):
@@ -266,7 +273,7 @@
     def block_of(ref, b):
         return ref[pl.ds(b * TB, TB)].reshape(rhs, LANES)
 
-    def over_rows(mat, rows, width, target):
+    def over_rows(mat, rows, width, target, ready=None):
         step = min(512, width)
         for nt in range(width // step):
             def body(k, acc):
@@ -279,6 +286,9 @@
             acc = lax.fori_loop(0, rows // 256, body, jnp.zeros((rhs, step), jnp.float32), unroll=2 if rows >= 512 else 1)
             for c in range(step // LANES):
                 target[pl.ds((nt * (step // LANES) + c) * TB, TB)] = acc[:, c * LANES:(c + 1) * LANES].reshape(TB, SUB, LANES)
+            if ready is not None:
+                per = step // LANES * TB
+                ready(nt * per, (nt + 1) * per)
 
     def over_cols(mat, rows, width, target, chunk=None):
         step = min(512, width)
@@ -322,8 +332,10 @@
                 put_w(b // 2, b % 2, block_of(src[d], b))
         loads["i", d].wait()
         if G > 1:
-            over_rows(inv[d], nT // TB * LANES, cols[d], y_part)
-            group_sum(f"y{d}", group, y_part, cols[d] // LANES * TB, y_full[d])
+            group_sum(
+                f"y{d}", group, y_part, cols[d] // LANES * TB, y_full[d],
+                lambda ready: over_rows(inv[d], nT // TB * LANES, cols[d], y_part, ready),
+            )
         else:
             over_rows(inv[d], nT // TB * LANES, cols[d], y_full[d])
         fill_y(lambda cb: block_of(y_full[d], cb), d)
@@ -359,8 +371,10 @@
 
             lax.fori_loop(0, nb[d] // 2, gather, 0, unroll=2)
             if G > 1:
-                over_rows(upd[d], nb[d] * LANES, cols[d], y_part)
-                group_sum(f"s{d}", group, y_part, cols[d] // LANES * TB, s_full[d])
+                group_sum(
+                    f"s{d}", group, y_part, cols[d] // LANES * TB, s_full[d],
+                    lambda ready: over_rows(upd[d], nb[d] * LANES, cols[d], y_part, ready),
+                )
             else:
                 over_rows(upd[d], nb[d] * LANES, cols[d], s_full[d])
             fill_y(lambda cb: block_of(y_full[d], cb) - block_of(s_full[d], cb), d)

time: 160 us -> 158 us (0.988)
  no operation moved by 1% of the time
where the time goes in v3:
time: 158 us
  Pallas kernels  155 us (98%)
  other arithmetic  2.29 us (1%)
    pallas_call x1, Pallas kernels, body(): pl.pallas_call(functools.partial(kernel, cfg), name='solve', out_shape=[j...  153 us

profile of v3, /device:TPU:0, one launch (start us, length us, event | category | flops | bytes accessed | tf_op | source)
XLA Modules:
  0.0 158.2 jit_solution(291973416137281516)
XLA Ops:
  0.6 0.7 compare_select_fusion.2
  1.3 0.7 compare_select_fusion.5
  2.0 0.1 select_reduce_fusion.2
  2.1 0.7 compare_select_fusion.4
  2.7 0.1 select_reduce_fusion.1
  2.8 0.1 select_reduce_fusion
  2.9 0.7 concatenate.3.refs_0_
  3.6 152.7 %solve.1 = (f32[32,8,128]{2,1,0:T(8,128)}, f32[32,8,128]{2,1,0:T(8,128)}, f32[32,8,128]{2,1,0:T(8,128)}, f32[32,8,128]{2,1,0:T(8,128)}) custom-call(s32[352]{0:T(512)} %concatenate.3.refs_0_, f32[32,8,128]{2,1,0:T(8,128)} %bitcast.22, f32[32,8,128]{2,1,0:T(8,128)} %bitcast.23, f32[32,8,128]{2,1,0:T(8,128)} %bitcast.24, f32[32,8,128]{2,1,0:T(8,128)} %bitcast.25, ...), custom_call_target="tpu_custom_call" | custom-call | tf_op jit(solution)/shard_map/solve/pallas_call | solution.py:488
  156.3 1.9 %hand_over.1 = (f32[32,8,128]{2,1,0:T(8,128)}, f32[32,8,128]{2,1,0:T(8,128)}, f32[32,8,128]{2,1,0:T(8,128)}, f32[32,8,128]{2,1,0:T(8,128)}) custom-call(f32[32,8,128]{2,1,0:T(8,128)} %get-tuple-element.12.refs_0_, f32[32,8,128]{2,1,0:T(8,128)} %get-tuple-element.13.refs_1_, f32[32,8,128]{2,1,0:T(8,128)} %get-tuple-element.14.refs_2_, ...), custom_call_target="tpu_custom_call" | custom-call | tf_op jit(solution)/shard_map/hand_over/pallas_call | solution.py:499
  (3 shorter events, 0.0 us)
